TPU v7x, 256 devices: a whole 4x4x8 slice. The times are simulated.
256 devices in a mesh: sx: 4 (over x_lo, core), sy: 8 (over z), ch: 8 (over x_hi, y).
Axes of the slice: x: 4 (x_hi: 2, x_lo: 2; x = x_hi * 2 + x_lo), y: 4, z: 8, core: 2. Of those that a mesh axis runs over, the one named last changes fastest.
Arguments:
- volume: bfloat16 [512, 32, 1024], P('ch', 'sx', 'sy'), may hold values from -6 to 6
- weight: bfloat16 [3, 3, 3, 512, 512], P(None, None, None, 'ch'), may hold values from -0.0546875 to 0.0546875
- bias: float32 [512], P('ch'), may hold values from -3 to 3
Outputs:
- convolved: bfloat16 [512, 32, 1024], P('ch', 'sx', 'sy')
All inputs are finite; a program needn't handle non-finite values.
Results may differ from a plain program's by a relative error of at most 0.001.
Values may be sent and summed in bfloat16 or wider, within the bound.
A program may use at most 192 MiB of HBM per device.

v0:
```python
import jax
import jax.numpy as jnp
from jax import lax
from jax.sharding import PartitionSpec as P

CZ = 16


def padded(cells, sides, width):
    for axis, dim in sides:
        count = lax.axis_size(axis)
        ends = count - 1
        head = lax.slice_in_dim(cells, 0, width, axis=dim)
        tail = lax.slice_in_dim(cells, cells.shape[dim] - width, cells.shape[dim], axis=dim)
        cells = jnp.concatenate(
            [
                lax.ppermute(tail, axis, [(i, (i + 1) % count) for i in range(ends)]),
                cells,
                lax.ppermute(head, axis, [((i + 1) % count, i) for i in range(ends)]),
            ],
            axis=dim,
        )
    return cells


def add_taps(running, extended, filters, cells_x, cells_y, cells_z):
    channels = extended.shape[0]
    outputs = running.shape[0]
    count = cells_x * cells_y * cells_z
    for along_x in range(3):
        for along_y in range(3):
            window = extended[:, along_x : along_x + cells_x, along_y : along_y + cells_y, :]
            window = window.reshape(channels, count)
            for along_z in range(3):
                tap_matrix = filters[along_x, along_y, along_z]
                product = jnp.dot(tap_matrix, window, preferred_element_type=jnp.float32)
                product = product.reshape(outputs, cells_x, cells_y, cells_z)
                if along_z == 0:
                    edge = jnp.zeros_like(product[..., :1])
                    product = jnp.concatenate([edge, product[..., :-1]], axis=3)
                elif along_z == 2:
                    edge = jnp.zeros_like(product[..., :1])
                    product = jnp.concatenate([product[..., 1:], edge], axis=3)
                running = running + product
    return running


def per_device(volume, weight, bias):
    local_in, cells_x, merged = volume.shape
    cells_z = CZ
    cells_y = merged // cells_z
    local_out = weight.shape[3]
    blocked = volume.reshape(local_in, cells_x, cells_y, cells_z)
    starting = jnp.zeros((local_out, cells_x, cells_y, cells_z), jnp.float32)
    gathered = lax.all_gather(blocked, "ch", axis=0, tiled=True)
    extended = padded(gathered, (("sx", 1), ("sy", 2)), 1)
    summed = add_taps(starting, extended, weight, cells_x, cells_y, cells_z)
    result = (summed + bias[:, None, None, None]).reshape(local_out, cells_x, cells_y * cells_z)
    return result.astype(jnp.bfloat16)


def solution(mesh):
    return jax.shard_map(
        per_device,
        mesh=mesh,
        in_specs=(P("ch", "sx", "sy"), P(None, None, None, "ch", None), P("ch")),
        out_specs=P("ch", "sx", "sy"),
        check_vma=False,
    )
```

profile of v0, /device:TPU:97, one launch (start us, length us, event | category | flops | bytes accessed | tf_op | source)
XLA Modules:
  0.0 237.1 jit_solution(625560326994363568)
XLA Ops:
  7.6 2.6 %copy.90 = bf16[64,8,8,16]{3,2,1,0:T(8,128)(2,1)} copy(bf16[64,8,8,16]{0,3,2,1:T(8,128)(2,1)S(1)} %bitcast.265) | data formatting | bytes 262144 | tf_op jit(solution)/shard_map/reshape | solution.py:53
  10.3 113.8 %all-gather.2.cloned.1.call-done = bf16[512,8,8,16]{3,2,1,0:T(8,128)(2,1)} async-done(((bf16[64,8,8,16]{3,2,1,0:T(8,128)(2,1)}), bf16[512,8,8,16]{3,2,1,0:T(8,128)(2,1)}) %all-gather.2.cloned.1.call-update) | async-done | bytes 1048592 | tf_op jit(solution)/shard_map/all_gather | solution.py:55
  124.1 8.3 %copy.91 = bf16[512,8,8,16]{0,3,2,1:T(8,128)(2,1)S(1)} copy(bf16[512,8,8,16]{3,2,1,0:T(8,128)(2,1)} %all-gather.2.cloned.1.call-done) | data formatting | bytes 2097152 | tf_op jit(solution)/shard_map/all_gather | solution.py:55
  132.4 3.2 %collective-permute-start = (bf16[512,1,8,16]{0,3,2,1:T(8,128)(2,1)S(1)}, bf16[512,1,8,16]{0,3,2,1:T(8,128)(2,1)S(1)}, u32[]{:S(2)}, u32[]{:S(2)}) collective-permute-start(bf16[512,1,8,16]{0,3,2,1:T(8,128)(2,1)S(1)} %get-tuple-element.17), channel_id=1, source_target_pairs={{0,64},{64,128},{128,192},{1,65},{65,129},{129,193},{2,66},{66,130... | collective-permute-start | bytes 393224 | tf_op jit(solution)/shard_map/ppermute | solution.py:17
  135.5 1.9 collective-permute-start.1
  137.5 2.1 fusion.15
  143.3 2.0 convolution_bitcast_fusion.19
  145.3 2.0 convolution_bitcast_fusion.3
  147.2 2.0 convolution_bitcast_fusion.5
  149.2 2.0 convolution_bitcast_fusion.20
  152.0 4.4 %collective-permute-start.2 = (bf16[512,10,1,16]{0,3,2,1:T(8,128)(2,1)}, bf16[512,10,1,16]{0,3,2,1:T(8,128)(2,1)}, u32[]{:S(2)}, u32[]{:S(2)}) collective-permute-start(bf16[512,10,1,16]{0,3,2,1:T(8,128)(2,1)} %get-tuple-element.13), channel_id=1, source_target_pairs={{0,8},{8,16},{16,24},{24,32},{32,40},{40,48},{48,56},{1,9},{9,17},... | collective-permute-start | bytes 491528 | tf_op jit(solution)/shard_map/ppermute | solution.py:17
  156.4 2.1 collective-permute-start.3
  160.6 2.0 copy.117
  162.5 1.9 slice.260
  164.4 2.0 copy.99
  166.4 2.0 copy.115
  168.4 1.9 copy.98
  170.3 2.0 convolution_bitcast_fusion.4
  172.3 2.0 copy.116
  212.9 2.0 copy.94
  217.9 1.9 copy.95
  219.8 1.9 copy.112
  221.8 2.0 copy.119
  223.7 5.7 %fusion.14 = bf16[64,8,8,16]{0,3,2,1:T(8,128)(2,1)S(1)} fusion(f32[64,8,8,16]{0,3,2,1:T(8,128)} %bitcast.255, f32[64,8,8,16]{0,3,2,1:T(8,128)} %bitcast.243, f32[64,8,8,16]{0,3,2,1:T(8,128)} %bitcast.254, f32[64,8,8,16]{0,3,2,1:T(8,128)} %bitcast.252, f32[64,8,8,15]{0,3,2,1:T(8,128)} %slice.263, f32[64,8,8,15]{0,3,2,1:T(8,128)} %bitcast.244, ...), kind=kOutput, calls=%fused_computation.17 | convolution fusion | flops 68943872 | bytes 13779200 | tf_op jit(solution)/shard_map/dot_general | solution.py:36
  (73 shorter events, 50.1 us)
Async XLA Ops:
  6.5 117.5 %all-gather.2.cloned.1.call-start = ((), (), s32[]{:S(2)}) async-start(), calls=%async_computation | async-start | bytes 9437184 | tf_op jit(solution)/shard_map/all_gather | solution.py:55
  132.4 8.4 %collective-permute-start = (bf16[512,1,8,16]{0,3,2,1:T(8,128)(2,1)S(1)}, bf16[512,1,8,16]{0,3,2,1:T(8,128)(2,1)S(1)}, u32[]{:S(2)}, u32[]{:S(2)}) collective-permute-start(bf16[512,1,8,16]{0,3,2,1:T(8,128)(2,1)S(1)} %get-tuple-element.17), channel_id=1, source_target_pairs={{0,64},{64,128},{128,192},{1,65},{65,129},{129,193},{2,66},{66,130... | collective-permute-start | bytes 393224 | tf_op jit(solution)/shard_map/ppermute | solution.py:17
  135.5 6.3 %collective-permute-start.1 = (bf16[512,1,8,16]{0,3,2,1:T(8,128)(2,1)S(1)}, bf16[512,1,8,16]{0,3,2,1:T(8,128)(2,1)S(1)}, u32[]{:S(2)}, u32[]{:S(2)}) collective-permute-start(bf16[512,1,8,16]{0,3,2,1:T(8,128)(2,1)S(1)} %get-tuple-element.18), channel_id=1, source_target_pairs={{64,0},{128,64},{192,128},{65,1},{129,65},{193,129},{66,2},{130,66... | collective-permute-start | bytes 393224 | tf_op jit(solution)/shard_map/ppermute | solution.py:19
  152.0 22.3 %collective-permute-start.2 = (bf16[512,10,1,16]{0,3,2,1:T(8,128)(2,1)}, bf16[512,10,1,16]{0,3,2,1:T(8,128)(2,1)}, u32[]{:S(2)}, u32[]{:S(2)}) collective-permute-start(bf16[512,10,1,16]{0,3,2,1:T(8,128)(2,1)} %get-tuple-element.13), channel_id=1, source_target_pairs={{0,8},{8,16},{16,24},{24,32},{32,40},{40,48},{48,56},{1,9},{9,17},... | collective-permute-start | bytes 491528 | tf_op jit(solution)/shard_map/ppermute | solution.py:17
  156.4 17.9 %collective-permute-start.3 = (bf16[512,10,1,16]{0,3,2,1:T(8,128)(2,1)}, bf16[512,10,1,16]{0,3,2,1:T(8,128)(2,1)}, u32[]{:S(2)}, u32[]{:S(2)}) collective-permute-start(bf16[512,10,1,16]{0,3,2,1:T(8,128)(2,1)} %get-tuple-element.14), channel_id=1, source_target_pairs={{8,0},{16,8},{24,16},{32,24},{40,32},{48,40},{56,48},{9,1},{17,9},... | collective-permute-start | bytes 491528 | tf_op jit(solution)/shard_map/ppermute | solution.py:19
  175.7 1.5 copy-start.2
  207.7 3.0 %copy-start.3 = (f32[64,1024]{1,0:T(8,128)S(1)}, f32[64,1024]{1,0:T(8,128)}, u32[]{:S(2)}) copy-start(f32[64,1024]{1,0:T(8,128)} %convolution_bitcast_fusion.14) | copy-start | bytes 786436
  207.7 4.1 %copy-start.4 = (f32[64,1024]{1,0:T(8,128)S(1)}, f32[64,1024]{1,0:T(8,128)}, u32[]{:S(2)}) copy-start(f32[64,1024]{1,0:T(8,128)} %convolution_bitcast_fusion.17) | copy-start | bytes 786436
  209.7 5.1 %copy-start.5 = (f32[64,1024]{1,0:T(8,128)S(1)}, f32[64,1024]{1,0:T(8,128)}, u32[]{:S(2)}) copy-start(f32[64,1024]{1,0:T(8,128)} %convolution_bitcast_fusion.16) | copy-start | bytes 786436
  210.7 5.1 %copy-start.6 = (f32[64,1024]{1,0:T(8,128)S(1)}, f32[64,1024]{1,0:T(8,128)}, u32[]{:S(2)}) copy-start(f32[64,1024]{1,0:T(8,128)} %convolution_bitcast_fusion.13) | copy-start | bytes 786436
  211.8 5.1 %copy-start.7 = (f32[64,1024]{1,0:T(8,128)S(1)}, f32[64,1024]{1,0:T(8,128)}, u32[]{:S(2)}) copy-start(f32[64,1024]{1,0:T(8,128)} %convolution_bitcast_fusion.10) | copy-start | bytes 786436
  216.9 6.9 %copy-start = (f32[64,8,8,15]{0,3,2,1:T(8,128)S(1)}, f32[64,8,8,15]{0,3,2,1:T(8,128)}, u32[]{:S(2)}) copy-start(f32[64,8,8,15]{0,3,2,1:T(8,128)} %slice.260) | copy-start | bytes 737284
  216.9 6.9 %copy-start.1 = (f32[64,1024]{0,1:T(8,128)S(1)}, f32[64,1024]{0,1:T(8,128)}, u32[]{:S(2)}) copy-start(f32[64,1024]{0,1:T(8,128)} %copy.99) | copy-start | bytes 786436
  216.9 6.9 %copy-start.8 = (f32[64]{0:T(128)S(1)}, f32[64]{0:T(128)}, u32[]{:S(2)}) copy-start(f32[64]{0:T(128)} %param.5) | copy-start | bytes 772
Sparse Core Ops, SparseCore 0:
  10.4 113.5 all-gather.1
where the time goes:
time: 239 us; the launch traced here: 237 us
  waiting for transfers between devices  115 us (48%)
  local copies, waits for them, and re-layouts  56.1 us (23%)
  matrix products  38.7 us (16%)
  between operations  13.6 us (6%)
  starting transfers between devices  11.6 us (5%)
    all_gather x1, waiting for transfers between devices, per_device(): gathered = lax.all_gather(blocked, 'ch', axis=0, tiled=True)  114 us
    dot_general x27, matrix products, add_taps(): product = jnp.dot(tap_matrix, window, preferred_element_type=jnp.float32)  38.7 us
    dot_general x24, local copies, waits for them, and re-layouts, add_taps(): product = jnp.dot(tap_matrix, window, preferred_element_type=jnp.float32)  33.7 us
    all_gather x1, local copies, waits for them, and re-layouts, per_device(): gathered = lax.all_gather(blocked, 'ch', axis=0, tiled=True)  8.27 us
    slice x8, local copies, waits for them, and re-layouts, add_taps(): product = jnp.concatenate([product[..., 1:], edge], axis=3)  8.07 us
    ppermute x2, starting transfers between devices, padded(): lax.ppermute(tail, axis, [(i, (i + 1) % count) for i in range(ends)])  7.54 us
  transfers between devices with their start and end apart: 5, of which 2 were waited for; matrix products, arithmetic and copies ran while one was open for 8% of the time, Pallas kernels for 0%

commit v1 on v0

v1 whole, which is shorter than its diff:
```python
import jax
import jax.numpy as jnp
from jax import lax
from jax.experimental import pallas as pl
from jax.experimental.pallas import tpu as pltpu
from jax.sharding import PartitionSpec as P

CZ = 16
LANES = 128
MESH = pl.DeviceIdType.MESH
F32 = jnp.float32
BF16 = jnp.bfloat16


def kernel(sizes, v_hbm, w_hbm, b_ref, o_ref, X, W, V, acc, flat, hx, hy, hc, rx, ry, rc,
           load_sem, gs, gr, hs, hr):
    n_sx, n_sy, n_ch = sizes
    half_ch = n_ch // 2
    cin, cells_x = V.shape[0], V.shape[1]
    cout = W.shape[3]
    group = half_ch * cin
    sx, sy, ch = lax.axis_index("sx"), lax.axis_index("sy"), lax.axis_index("ch")
    h, y = ch // half_ch, lax.rem(ch, half_ch)

    def member(other, dy):
        return jnp.where(other == 1, 1 - h, h) * half_ch + lax.rem(y + dy, half_ch)

    def mate(other, dy):
        return (sx, sy, member(other, dy))

    def spatial(dx, dy):
        return (lax.rem(sx + dx + n_sx, n_sx), lax.rem(sy + dy + n_sy, n_sy), ch)

    load_v = pltpu.make_async_copy(v_hbm, V, load_sem.at[0])
    load_w = pltpu.make_async_copy(w_hbm, W, load_sem.at[1])
    load_v.start()
    load_w.start()

    barrier = pltpu.get_barrier_semaphore()
    mates = [(0, 1), (0, half_ch - 1), (0, 2), (1, 0)]
    spots = [(dx, dy) for dx in (-1, 0, 1) for dy in (-1, 0, 1) if (dx, dy) != (0, 0)]
    for m in mates:
        pl.semaphore_signal(barrier, inc=1, device_id=mate(*m), device_id_type=MESH)
    for s in spots:
        pl.semaphore_signal(barrier, inc=1, device_id=spatial(*s), device_id_type=MESH)

    lane = lax.broadcasted_iota(jnp.int32, (cin, LANES), 1)
    z = lax.rem(lane, CZ)

    load_v.wait()
    flat[...] = V[...].astype(F32).reshape(cin * cells_x, LANES)

    def rows(who):
        return pl.ds(pl.multiple_of(who * cin, cin), cin)

    zero = jnp.zeros((group * 2, LANES), BF16)
    for c in range(3):
        X[c, 0] = zero
        X[c, cells_x + 1] = zero

    mine = rows(ch)
    for x in range(cells_x):
        X[1, x + 1, mine, :] = flat[pl.ds(x, cin, stride=cells_x), :].astype(BF16)

    def shift_z(who):
        r = rows(who)
        for x in range(1, cells_x + 1):
            v = X[1, x, r, :]
            X[0, x, r, :] = jnp.where(z == 0, jnp.zeros_like(v), pltpu.roll(v, 1, 1))
            X[2, x, r, :] = jnp.where(z == CZ - 1, jnp.zeros_like(v), pltpu.roll(v, LANES - 1, 1))

    def send(who, slot, to):
        block = X.at[1, 1 : cells_x + 1, rows(who), :]
        copy = pltpu.make_async_remote_copy(
            src_ref=block, dst_ref=block, send_sem=gs.at[slot], recv_sem=gr.at[slot],
            device_id=to, device_id_type=MESH)
        copy.start()
        return copy

    def arrived(other, dy):
        slot = other * half_ch + dy
        block = X.at[1, 1 : cells_x + 1, rows(member(other, dy)), :]
        pltpu.make_async_remote_copy(
            src_ref=block, dst_ref=block, send_sem=gs.at[slot], recv_sem=gr.at[slot],
            device_id=mate(other, 0), device_id_type=MESH).wait_recv()

    pl.semaphore_wait(barrier, len(mates) + len(spots))
    sent = []
    sent.append(send(ch, half_ch + 0, mate(1, 0)))
    sent.append(send(ch, half_ch - 1, mate(0, 1)))
    sent.append(send(ch, 1, mate(0, half_ch - 1)))
    sent.append(send(ch, 2, mate(0, 2)))
    shift_z(ch)
    arrived(1, 0)
    sent.append(send(member(1, 0), half_ch + half_ch - 1, mate(0, 1)))
    sent.append(send(member(1, 0), half_ch + 1, mate(0, half_ch - 1)))
    shift_z(member(1, 0))
    arrived(0, 1)
    shift_z(member(0, 1))
    arrived(0, half_ch - 1)
    shift_z(member(0, half_ch - 1))
    arrived(0, 2)
    sent.append(send(member(0, 2), half_ch + 2, mate(1, 0)))
    shift_z(member(0, 2))
    load_w.wait()

    def products(which, first):
        cols = pl.ds(pl.multiple_of(which * group, group), group)
        for p in range((cells_x + 2) // 2):
            taps = [a for a in range(3) if 0 < 2 * p + a and 2 * p + a - 1 < cells_x + 1]
            lhs = jnp.concatenate(
                [W[a, :, c, :, cols].reshape(3 * cout, group) for a in taps for c in range(3)], axis=1)
            rhs = jnp.concatenate(
                [jnp.concatenate([X[c, 2 * p + a - 1, cols, :], X[c, 2 * p + a, cols, :]], axis=1)
                 for a in taps for c in range(3)], axis=0)
            r = jnp.dot(lhs, rhs, preferred_element_type=F32)
            for j in range(2):
                part = r[:, LANES * j : LANES * (j + 1)]
                if first:
                    acc[2 * p + j] = part
                else:
                    acc[2 * p + j] = acc[2 * p + j] + part

    products(h, True)
    arrived(1, 1)
    shift_z(member(1, 1))
    arrived(1, half_ch - 1)
    shift_z(member(1, half_ch - 1))
    arrived(1, 2)
    shift_z(member(1, 2))
    products(1 - h, False)

    lane_o = lax.broadcasted_iota(jnp.int32, (cout, LANES), 1)
    last = LANES - CZ

    def taps_of(s, b):
        return acc[s, b * cout : (b + 1) * cout]

    def along_y(s):
        up = jnp.where(lane_o < CZ, 0.0, pltpu.roll(taps_of(s, 0), CZ, 1))
        down = jnp.where(lane_o >= last, 0.0, pltpu.roll(taps_of(s, 2), LANES - CZ, 1))
        return taps_of(s, 1) + up + down

    def roll(v, by):
        by = by % LANES
        return pltpu.roll(v, by, 1) if by else v

    hx[0] = along_y(0)
    hx[1] = along_y(cells_x + 1)
    low = jnp.zeros((cout, LANES), F32)
    high = jnp.zeros((cout, LANES), F32)
    for x in range(cells_x):
        here = (lane_o >= x * CZ) & (lane_o < (x + 1) * CZ)
        low = jnp.where(here, roll(taps_of(x + 1, 2), x * CZ), low)
        high = jnp.where(here, roll(taps_of(x + 1, 0), x * CZ - last), high)
    hy[0] = low
    hy[1] = high
    rows_of = cout // 8
    lane_8 = lax.broadcasted_iota(jnp.int32, (8, LANES), 1)
    for i, s in enumerate((0, cells_x + 1)):
        for j, (b, start) in enumerate(((2, 0), (0, last))):
            corner = jnp.zeros((8, LANES), F32)
            for g in range(rows_of):
                here = (lane_8 >= g * CZ) & (lane_8 < (g + 1) * CZ)
                piece = acc[s, b * cout + 8 * g : b * cout + 8 * g + 8]
                corner = jnp.where(here, roll(piece, g * CZ - start), corner)
            hc[2 * i + j] = corner

    def give(src, dst, slot, to):
        copy = pltpu.make_async_remote_copy(
            src_ref=src, dst_ref=dst, send_sem=hs.at[slot], recv_sem=hr.at[slot],
            device_id=to, device_id_type=MESH)
        copy.start()
        return copy

    halos = []
    for i, d in enumerate((-1, 1)):
        halos.append(give(hy.at[i], ry.at[i], 2 + i, spatial(0, d)))
    for i, d in enumerate((-1, 1)):
        halos.append(give(hx.at[i], rx.at[i], i, spatial(d, 0)))
    for i, dx in enumerate((-1, 1)):
        for j, dy in enumerate((-1, 1)):
            k = 2 * i + j
            halos.append(give(hc.at[k], rc.at[k], 4 + k, spatial(dx, dy)))

    sub = lax.broadcasted_iota(jnp.int32, (cout, cout), 0)
    across = lax.broadcasted_iota(jnp.int32, (cout, cout), 1)
    bias = jnp.sum(jnp.where(sub == across, jnp.broadcast_to(b_ref[...], (cout, cout)), 0.0),
                   axis=1, keepdims=True)
    for x in range(cells_x):
        flat[pl.ds(x, cout, stride=cells_x), :] = along_y(x + 1) + bias

    for copy in halos:
        copy.wait()
    has = (sx > 0, sx < n_sx - 1)
    has_y = (sy > 0, sy < n_sy - 1)
    zeros = jnp.zeros((cout, LANES), F32)
    from_low_y = jnp.where(has_y[0], ry[1], zeros)
    from_high_y = jnp.where(has_y[1], ry[0], zeros)
    for x in range(cells_x):
        extra = jnp.where(lane_o < CZ, roll(from_low_y, -x * CZ), 0.0)
        extra = jnp.where(lane_o >= last, roll(from_high_y, last - x * CZ), extra)
        if x in (0, cells_x - 1):
            i = 0 if x == 0 else 1
            extra = extra + jnp.where(has[i], rx[1 - i], zeros)
            corners = []
            for j in range(2):
                start = 0 if j == 0 else last
                packed = jnp.where(has[i] & has_y[j], rc[2 * (1 - i) + 1 - j], jnp.zeros((8, LANES), F32))
                spread = jnp.concatenate([roll(packed, start - g * CZ) for g in range(rows_of)], axis=0)
                inside = lane_o < CZ if j == 0 else lane_o >= last
                extra = extra + jnp.where(inside, spread, 0.0)
        spot = pl.ds(x, cout, stride=cells_x)
        flat[spot, :] = flat[spot, :] + extra
    o_ref[...] = flat[...].reshape(cout, cells_x, LANES).astype(BF16)
    for copy in sent:
        copy.wait_send()


def solution(mesh):
    sizes = tuple(mesh.shape[a] for a in ("sx", "sy", "ch"))
    n_ch = sizes[2]

    def per_device(volume, weight, bias):
        cin, cells_x, merged = volume.shape
        cout = weight.shape[3]
        call = pl.pallas_call(
            lambda *refs: kernel(sizes, *refs),
            out_shape=jax.ShapeDtypeStruct((cout, cells_x, merged), BF16),
            in_specs=[
                pl.BlockSpec(memory_space=pl.ANY),
                pl.BlockSpec(memory_space=pl.ANY),
                pl.BlockSpec(memory_space=pltpu.VMEM),
            ],
            out_specs=pl.BlockSpec(memory_space=pltpu.VMEM),
            scratch_shapes=[
                pltpu.VMEM((3, cells_x + 2, n_ch * cin, LANES), BF16),
                pltpu.VMEM(weight.shape, BF16),
                pltpu.VMEM((cin, cells_x, LANES), BF16),
                pltpu.VMEM((cells_x + 2, 3 * cout, LANES), F32),
                pltpu.VMEM((cout * cells_x, LANES), F32),
                pltpu.VMEM((2, cout, LANES), F32),
                pltpu.VMEM((2, cout, LANES), F32),
                pltpu.VMEM((4, 8, LANES), F32),
                pltpu.VMEM((2, cout, LANES), F32),
                pltpu.VMEM((2, cout, LANES), F32),
                pltpu.VMEM((4, 8, LANES), F32),
                pltpu.SemaphoreType.DMA((2,)),
                pltpu.SemaphoreType.DMA((n_ch,)),
                pltpu.SemaphoreType.DMA((n_ch,)),
                pltpu.SemaphoreType.DMA((8,)),
                pltpu.SemaphoreType.DMA((8,)),
            ],
            compiler_params=pltpu.CompilerParams(
                collective_id=0, has_side_effects=True, vmem_limit_bytes=48 << 20),
            name="conv_gather",
        )
        return call(volume, weight, bias.reshape(1, cout))

    return jax.shard_map(
        per_device,
        mesh=mesh,
        in_specs=(P("ch", "sx", "sy"), P(None, None, None, "ch", None), P("ch")),
        out_specs=P("ch", "sx", "sy"),
        check_vma=False,
    )
```

time: 239 us -> 33.4 us (0.14)
  the two profiles are of different devices: /device:TPU:97 before, /device:TPU:1 now
where the time goes in v1:
time: 33.4 us; the launch traced here: 33.3 us
  Pallas kernels  29.6 us (89%)
  local copies, waits for them, and re-layouts  3.69 us (11%)
    pallas_call x1, Pallas kernels, per_device(): return call(volume, weight, bias.reshape(1, cout))  29.6 us
    unnamed x7, local copies, waits for them, and re-layouts  3.69 us

profile of v1, /device:TPU:1, one launch (start us, length us, event | category | flops | bytes accessed | tf_op | source)
XLA Modules:
  0.0 33.3 jit_solution(17639435123566831560)
XLA Ops:
  0.0 0.0 copy-start
  0.0 1.5 %copy-done = bf16[3,3,3,64,512]{4,3,2,1,0:T(8,128)(2,1)S(1)} copy-done((bf16[3,3,3,64,512]{4,3,2,1,0:T(8,128)(2,1)S(1)}, bf16[3,3,3,64,512]{4,3,2,1,0:T(8,128)(2,1)}, u32[]{:S(2)}) %copy-start) | copy-done | bytes 1769496
  1.5 0.0 copy-start.1
  1.5 0.9 %copy-done.1 = bf16[64,8,128]{2,1,0:T(8,128)(2,1)S(1)} copy-done((bf16[64,8,128]{2,1,0:T(8,128)(2,1)S(1)}, bf16[64,8,128]{2,1,0:T(8,128)(2,1)}, u32[]{:S(2)}) %copy-start.1) | copy-done | bytes 131096
  2.4 0.0 copy-start.2
  2.4 0.7 %copy-done.2 = f32[64]{0:T(128)S(1)} copy-done((f32[64]{0:T(128)S(1)}, f32[64]{0:T(128)}, u32[]{:S(2)}) %copy-start.2) | copy-done | bytes 280
  3.0 29.6 %conv_gather.1 = bf16[64,8,128]{2,1,0:T(8,128)(2,1)S(1)} custom-call(bf16[64,8,128]{2,1,0:T(8,128)(2,1)S(1)} %copy-done.1, bf16[3,3,3,64,512]{4,3,2,1,0:T(8,128)(2,1)S(1)} %copy-done, f32[1,64]{1,0:T(1,128)S(1)} %bitcast.1), custom_call_target="tpu_custom_call" | custom-call | tf_op jit(solution)/shard_map/conv_gather/pallas_call | solution.py:258
  32.6 0.7 %copy.5 = bf16[64,8,128]{2,1,0:T(8,128)(2,1)} copy(bf16[64,8,128]{2,1,0:T(8,128)(2,1)S(1)} %conv_gather.1) | data formatting | bytes 262144
Async XLA Ops:
  0.0 1.5 %copy-start = (bf16[3,3,3,64,512]{4,3,2,1,0:T(8,128)(2,1)S(1)}, bf16[3,3,3,64,512]{4,3,2,1,0:T(8,128)(2,1)}, u32[]{:S(2)}) copy-start(bf16[3,3,3,64,512]{4,3,2,1,0:T(8,128)(2,1)} %refs_1_.1) | copy-start | bytes 5308420
  1.5 0.9 %copy-start.1 = (bf16[64,8,128]{2,1,0:T(8,128)(2,1)S(1)}, bf16[64,8,128]{2,1,0:T(8,128)(2,1)}, u32[]{:S(2)}) copy-start(bf16[64,8,128]{2,1,0:T(8,128)(2,1)} %refs_0_.1) | copy-start | bytes 393220
  2.4 0.7 %copy-start.2 = (f32[64]{0:T(128)S(1)}, f32[64]{0:T(128)}, u32[]{:S(2)}) copy-start(f32[64]{0:T(128)} %param.5) | copy-start | bytes 772

commit v2 on v1

v2 whole, which is shorter than its diff:
```python
import jax
import jax.numpy as jnp
from jax import lax
from jax.experimental import pallas as pl
from jax.experimental.pallas import tpu as pltpu
from jax.sharding import PartitionSpec as P

CZ = 16
LANES = 128
MESH = pl.DeviceIdType.MESH
PARTS = 1
PLAN = [
    ("send", (0, 0), 0, (1, 0)),
    ("send", (0, 0), 0, (0, 1)),
    ("send", (0, 0), 0, (0, 3)),
    ("send", (0, 0), 0, (0, 2)),
    ("own",),
    ("wait", (1, 0), 0),
    ("send", (1, 0), 0, (0, 1)),
    ("send", (1, 0), 0, (0, 3)),
    ("wait", (0, 1), 0),
    ("wait", (0, 3), 0),
    ("wait", (0, 2), 0),
    ("send", (0, 2), 0, (1, 0)),
    ("first",),
    ("wait", (1, 1), 0),
    ("wait", (1, 3), 0),
    ("wait", (1, 2), 0),
    ("second",),
]
F32 = jnp.float32
BF16 = jnp.bfloat16


def kernel(sizes, v_hbm, w_hbm, b_hbm, o_ref, X, W, V, B, acc, flat, hx, hy, hc, rx, ry, rc,
           load_sem, gs, gr, hs, hr):
    n_sx, n_sy, n_ch = sizes
    half_ch = n_ch // 2
    cin, cells_x = V.shape[0], V.shape[1]
    cout = W.shape[3]
    group = half_ch * cin
    sx, sy, ch = lax.axis_index("sx"), lax.axis_index("sy"), lax.axis_index("ch")
    h, y = ch // half_ch, lax.rem(ch, half_ch)

    def member(other, k):
        across = (y, y + 1 - 2 * lax.rem(y, 2), lax.rem(y + 2, 4), 3 - y)[k]
        return (1 - h if other else h) * half_ch + across

    def mate(other, k):
        return (sx, sy, member(other, k))

    def spatial(dx, dy):
        return (sx + dx, sy + dy, ch)

    has_x = {-1: sx > 0, 0: sx >= 0, 1: sx < n_sx - 1}
    has_y = {-1: sy > 0, 0: sy >= 0, 1: sy < n_sy - 1}

    def exists(dx, dy):
        return has_x[dx] & has_y[dy]

    load_v = pltpu.make_async_copy(v_hbm, V, load_sem.at[0])
    load_w = pltpu.make_async_copy(w_hbm, W, load_sem.at[1])
    load_b = pltpu.make_async_copy(b_hbm, B, load_sem.at[2])
    load_v.start()
    load_b.start()
    load_w.start()

    barrier = pltpu.get_barrier_semaphore()
    mates = sorted({step[3] for step in PLAN if step[0] == "send"})
    spots = [(dx, dy) for dx in (-1, 0, 1) for dy in (-1, 0, 1) if (dx, dy) != (0, 0)]
    for m in mates:
        pl.semaphore_signal(barrier, inc=1, device_id=mate(*m), device_id_type=MESH)
    for s in spots:

        @pl.when(exists(*s))
        def _():
            pl.semaphore_signal(barrier, inc=1, device_id=spatial(*s), device_id_type=MESH)

    across_x = jnp.where(has_x[-1], 1, 0) + jnp.where(has_x[1], 1, 0) + 1
    across_y = jnp.where(has_y[-1], 1, 0) + jnp.where(has_y[1], 1, 0) + 1
    n_spots = across_x * across_y - 1

    lane = lax.broadcasted_iota(jnp.int32, (cin, LANES), 1)
    z = lax.rem(lane, CZ)

    load_v.wait()
    flat[...] = V[...].astype(F32).reshape(cin * cells_x, LANES)

    def rows(who):
        return pl.ds(pl.multiple_of(who * cin, cin), cin)

    zero = jnp.zeros((group * 2, LANES), BF16)
    for c in range(3):
        X[c, 0] = zero
        X[c, cells_x + 1] = zero

    mine = rows(ch)
    for x in range(cells_x):
        X[1, x + 1, mine, :] = flat[pl.ds(x, cin, stride=cells_x), :].astype(BF16)

    def shift_z(who, xs):
        r = rows(who)
        for x in xs:
            v = X[1, x + 1, r, :]
            X[0, x + 1, r, :] = jnp.where(z == 0, jnp.zeros_like(v), pltpu.roll(v, 1, 1))
            X[2, x + 1, r, :] = jnp.where(z == CZ - 1, jnp.zeros_like(v), pltpu.roll(v, LANES - 1, 1))

    def block_copy(block, part, out, slot, to):
        width = cells_x // PARTS
        piece = X.at[1, 1 + part * width : 1 + (part + 1) * width, rows(member(*block)), :]
        return pltpu.make_async_remote_copy(
            src_ref=piece, dst_ref=piece, send_sem=gs.at[out], recv_sem=gr.at[slot],
            device_id=mate(*to), device_id_type=MESH)

    sent = []

    def send(block, part, to):
        other, k = block[0] ^ to[0], block[1] ^ to[1]
        copy = block_copy(block, part, len(sent), (other * half_ch + k) * PARTS + part, to)
        copy.start()
        sent.append(copy)

    def arrived(block, part):
        block_copy(block, part, 0, (block[0] * half_ch + block[1]) * PARTS + part, (1, 0)).wait_recv()

    def products(which, first):
        cols = pl.ds(pl.multiple_of(which * group, group), group)
        for p in range((cells_x + 2) // 2):
            taps = [a for a in range(3) if 0 < 2 * p + a and 2 * p + a - 1 < cells_x + 1]
            lhs = jnp.concatenate(
                [W[a, :, c, :, cols].reshape(3 * cout, group) for a in taps for c in range(3)], axis=1)
            rhs = jnp.concatenate(
                [jnp.concatenate([X[c, 2 * p + a - 1, cols, :], X[c, 2 * p + a, cols, :]], axis=1)
                 for a in taps for c in range(3)], axis=0)
            r = jnp.dot(lhs, rhs, preferred_element_type=F32)
            for j in range(2):
                part = r[:, LANES * j : LANES * (j + 1)]
                if first:
                    acc[2 * p + j] = part
                else:
                    acc[2 * p + j] = acc[2 * p + j] + part

    pl.semaphore_wait(barrier, len(mates) + n_spots)
    for step in PLAN:
        if step[0] == "send":
            send(*step[1:])
        elif step[0] == "wait":
            arrived(*step[1:])
            width = cells_x // PARTS
            shift_z(member(*step[1]), range(step[2] * width, (step[2] + 1) * width))
        elif step[0] == "own":
            shift_z(ch, range(cells_x))
        elif step[0] == "first":
            load_w.wait()
            load_b.wait()
            products(h, True)
        else:
            products(1 - h, False)

    lane_o = lax.broadcasted_iota(jnp.int32, (cout, LANES), 1)
    last = LANES - CZ

    def taps_of(s, b):
        return acc[s, b * cout : (b + 1) * cout]

    def along_y(s):
        up = jnp.where(lane_o < CZ, 0.0, pltpu.roll(taps_of(s, 0), CZ, 1))
        down = jnp.where(lane_o >= last, 0.0, pltpu.roll(taps_of(s, 2), LANES - CZ, 1))
        return taps_of(s, 1) + up + down

    def roll(v, by):
        by = by % LANES
        return pltpu.roll(v, by, 1) if by else v

    hx[0] = along_y(0)
    hx[1] = along_y(cells_x + 1)
    low = jnp.zeros((cout, LANES), F32)
    high = jnp.zeros((cout, LANES), F32)
    for x in range(cells_x):
        here = (lane_o >= x * CZ) & (lane_o < (x + 1) * CZ)
        low = jnp.where(here, roll(taps_of(x + 1, 2), x * CZ), low)
        high = jnp.where(here, roll(taps_of(x + 1, 0), x * CZ - last), high)
    hy[0] = low
    hy[1] = high
    rows_of = cout // 8
    lane_8 = lax.broadcasted_iota(jnp.int32, (8, LANES), 1)
    for i, s in enumerate((0, cells_x + 1)):
        for j, (b, start) in enumerate(((2, 0), (0, last))):
            corner = jnp.zeros((8, LANES), F32)
            for g in range(rows_of):
                here = (lane_8 >= g * CZ) & (lane_8 < (g + 1) * CZ)
                piece = acc[s, b * cout + 8 * g : b * cout + 8 * g + 8]
                corner = jnp.where(here, roll(piece, g * CZ - start), corner)
            hc[2 * i + j] = corner

    edges = [(hy.at[0], ry.at[0], 0, -1), (hy.at[1], ry.at[1], 0, 1),
             (hx.at[0], rx.at[0], -1, 0), (hx.at[1], rx.at[1], 1, 0)]
    edges += [(hc.at[2 * i + j], rc.at[2 * i + j], dx, dy)
              for i, dx in enumerate((-1, 1)) for j, dy in enumerate((-1, 1))]

    def edge_copy(k):
        src, dst, dx, dy = edges[k]
        return pltpu.make_async_remote_copy(
            src_ref=src, dst_ref=dst, send_sem=hs.at[k], recv_sem=hr.at[k],
            device_id=spatial(dx, dy), device_id_type=MESH)

    for k, (_, _, dx, dy) in enumerate(edges):

        @pl.when(exists(dx, dy))
        def _():
            edge_copy(k).start()

    sub = lax.broadcasted_iota(jnp.int32, (cout, cout), 0)
    across = lax.broadcasted_iota(jnp.int32, (cout, cout), 1)
    bias = jnp.sum(jnp.where(sub == across, jnp.broadcast_to(B[...], (cout, cout)), 0.0),
                   axis=1, keepdims=True)
    for x in range(cells_x):
        flat[pl.ds(x, cout, stride=cells_x), :] = along_y(x + 1) + bias

    for k, (_, _, dx, dy) in enumerate(edges):

        @pl.when(exists(-dx, -dy))
        def _():
            edge_copy(k).wait_recv()

    has, has_end = (has_x[-1], has_x[1]), (has_y[-1], has_y[1])
    zeros = jnp.zeros((cout, LANES), F32)
    from_low_y = jnp.where(has_end[0], ry[1], zeros)
    from_high_y = jnp.where(has_end[1], ry[0], zeros)
    for x in range(cells_x):
        extra = jnp.where(lane_o < CZ, roll(from_low_y, -x * CZ), 0.0)
        extra = jnp.where(lane_o >= last, roll(from_high_y, last - x * CZ), extra)
        if x in (0, cells_x - 1):
            i = 0 if x == 0 else 1
            extra = extra + jnp.where(has[i], rx[1 - i], zeros)
            corners = []
            for j in range(2):
                start = 0 if j == 0 else last
                packed = jnp.where(has[i] & has_end[j], rc[2 * (1 - i) + 1 - j], jnp.zeros((8, LANES), F32))
                spread = jnp.concatenate([roll(packed, start - g * CZ) for g in range(rows_of)], axis=0)
                inside = lane_o < CZ if j == 0 else lane_o >= last
                extra = extra + jnp.where(inside, spread, 0.0)
        spot = pl.ds(x, cout, stride=cells_x)
        flat[spot, :] = flat[spot, :] + extra
    o_ref[...] = flat[...].reshape(cout, cells_x, LANES).astype(BF16)
    for k, (_, _, dx, dy) in enumerate(edges):

        @pl.when(exists(dx, dy))
        def _():
            edge_copy(k).wait_send()

    for copy in sent:
        copy.wait_send()


def solution(mesh):
    sizes = tuple(mesh.shape[a] for a in ("sx", "sy", "ch"))
    n_ch = sizes[2]

    def per_device(volume, weight, bias):
        cin, cells_x, merged = volume.shape
        cout = weight.shape[3]
        call = pl.pallas_call(
            lambda *refs: kernel(sizes, *refs),
            out_shape=pltpu.VMEM((cout, cells_x, merged), BF16),
            in_specs=[
                pl.BlockSpec(memory_space=pltpu.HBM),
                pl.BlockSpec(memory_space=pltpu.HBM),
                pl.BlockSpec(memory_space=pltpu.HBM),
            ],
            out_specs=pl.BlockSpec(memory_space=pltpu.VMEM),
            scratch_shapes=[
                pltpu.VMEM((3, cells_x + 2, n_ch * cin, LANES), BF16),
                pltpu.VMEM(weight.shape, BF16),
                pltpu.VMEM((cin, cells_x, LANES), BF16),
                pltpu.VMEM((1, cout), F32),
                pltpu.VMEM((cells_x + 2, 3 * cout, LANES), F32),
                pltpu.VMEM((cout * cells_x, LANES), F32),
                pltpu.VMEM((2, cout, LANES), F32),
                pltpu.VMEM((2, cout, LANES), F32),
                pltpu.VMEM((4, 8, LANES), F32),
                pltpu.VMEM((2, cout, LANES), F32),
                pltpu.VMEM((2, cout, LANES), F32),
                pltpu.VMEM((4, 8, LANES), F32),
                pltpu.SemaphoreType.DMA((3,)),
                pltpu.SemaphoreType.DMA((n_ch * PARTS,)),
                pltpu.SemaphoreType.DMA((n_ch * PARTS,)),
                pltpu.SemaphoreType.DMA((8,)),
                pltpu.SemaphoreType.DMA((8,)),
            ],
            compiler_params=pltpu.CompilerParams(
                collective_id=0, has_side_effects=True, vmem_limit_bytes=32 << 20),
            name="conv_gather",
        )
        return call(*[pltpu.with_memory_space_constraint(a, pltpu.HBM) for a in (volume, weight, bias.reshape(1, cout))])

    return jax.shard_map(
        per_device,
        mesh=mesh,
        in_specs=(P("ch", "sx", "sy"), P(None, None, None, "ch", None), P("ch")),
        out_specs=P("ch", "sx", "sy"),
        check_vma=False,
    )
```

time: 33.4 us -> 27.3 us (0.82)
  the two profiles are of different devices: /device:TPU:1 before, /device:TPU:65 now
where the time goes in v2:
time: 27.3 us; the launch traced here: 27.2 us
  Pallas kernels  26.5 us (97%)
  local copies, waits for them, and re-layouts  0.66 us (2%)
    pallas_call x1, Pallas kernels, per_device(): call(*[pltpu.with_memory_space_constraint(a, pltpu.HBM) for a in (volume,...  26.5 us
    unnamed x1, local copies, waits for them, and re-layouts  0.66 us

profile of v2, /device:TPU:65, one launch (start us, length us, event | category | flops | bytes accessed | tf_op | source)
XLA Modules:
  0.0 27.2 jit_solution(17519745730745093175)
XLA Ops:
  0.0 26.5 %conv_gather.1 = bf16[64,8,128]{2,1,0:T(8,128)(2,1)S(1)} custom-call(bf16[64,8,128]{2,1,0:T(8,128)(2,1)} %refs_0_.1, bf16[3,3,3,64,512]{4,3,2,1,0:T(8,128)(2,1)} %refs_1_.1, f32[1,64]{1,0:T(1,128)} %bitcast.1), custom_call_target="tpu_custom_call" | custom-call | tf_op jit(solution)/shard_map/conv_gather/pallas_call | solution.py:295
  26.5 0.7 %copy.5 = bf16[64,8,128]{2,1,0:T(8,128)(2,1)} copy(bf16[64,8,128]{2,1,0:T(8,128)(2,1)S(1)} %conv_gather.1) | data formatting | bytes 262144

commit v3 on v2

--- a/solution.py
+++ b/solution.py
@@ -8,25 +8,39 @@
 CZ = 16
 LANES = 128
 MESH = pl.DeviceIdType.MESH
-PARTS = 1
+PARTS = 2
 PLAN = [
-    ("send", (0, 0), 0, (1, 0)),
-    ("send", (0, 0), 0, (0, 1)),
-    ("send", (0, 0), 0, (0, 3)),
-    ("send", (0, 0), 0, (0, 2)),
-    ("own",),
-    ("wait", (1, 0), 0),
-    ("send", (1, 0), 0, (0, 1)),
-    ("send", (1, 0), 0, (0, 3)),
-    ("wait", (0, 1), 0),
-    ("wait", (0, 3), 0),
-    ("wait", (0, 2), 0),
-    ("send", (0, 2), 0, (1, 0)),
-    ("first",),
-    ("wait", (1, 1), 0),
-    ("wait", (1, 3), 0),
-    ("wait", (1, 2), 0),
-    ("second",),
+    ('send', (0, 0), 0, (1, 0)),
+    ('send', (0, 0), 1, (0, 1)),
+    ('send', (0, 0), 0, (0, 3)),
+    ('send', (0, 0), 1, (1, 0)),
+    ('send', (0, 0), 0, (0, 1)),
+    ('send', (0, 0), 1, (0, 3)),
+    ('send', (0, 0), 0, (1, 2)),
+    ('send', (0, 0), 1, (1, 2)),
+    ('own',),
+    ('wait', (0, 1), 1),
+    ('send', (0, 1), 1, (0, 3)),
+    ('send', (0, 1), 1, (1, 0)),
+    ('wait', (0, 3), 0),
+    ('send', (0, 3), 0, (0, 1)),
+    ('send', (0, 3), 0, (1, 0)),
+    ('wait', (1, 0), 0),
+    ('send', (1, 0), 0, (0, 1)),
+    ('wait', (1, 0), 1),
+    ('send', (1, 0), 1, (0, 3)),
+    ('wait', (0, 1), 0),
+    ('wait', (0, 3), 1),
+    ('wait', (0, 2), 0),
+    ('wait', (0, 2), 1),
+    ('first',),
+    ('wait', (1, 1), 0),
+    ('wait', (1, 3), 0),
+    ('wait', (1, 1), 1),
+    ('wait', (1, 3), 1),
+    ('wait', (1, 2), 0),
+    ('wait', (1, 2), 1),
+    ('second',),
 ]
 F32 = jnp.float32
 BF16 = jnp.bfloat16

time: 27.3 us -> 24.8 us (0.908)
  the two profiles are of different devices: /device:TPU:65 before, /device:TPU:97 now
where the time goes in v3:
time: 24.8 us; the launch traced here: 24.7 us
  Pallas kernels  24 us (97%)
  local copies, waits for them, and re-layouts  0.66 us (3%)
    pallas_call x1, Pallas kernels, per_device(): call(*[pltpu.with_memory_space_constraint(a, pltpu.HBM) for a in (volume,...  24 us
    unnamed x1, local copies, waits for them, and re-layouts  0.66 us

profile of v3, /device:TPU:97, one launch (start us, length us, event | category | flops | bytes accessed | tf_op | source)
XLA Modules:
  0.0 24.7 jit_solution(8425332771878756522)
XLA Ops:
  0.0 24.0 %conv_gather.1 = bf16[64,8,128]{2,1,0:T(8,128)(2,1)S(1)} custom-call(bf16[64,8,128]{2,1,0:T(8,128)(2,1)} %refs_0_.1, bf16[3,3,3,64,512]{4,3,2,1,0:T(8,128)(2,1)} %refs_1_.1, f32[1,64]{1,0:T(1,128)} %bitcast.1), custom_call_target="tpu_custom_call" | custom-call | tf_op jit(solution)/shard_map/conv_gather/pallas_call | solution.py:309
  24.0 0.7 %copy.5 = bf16[64,8,128]{2,1,0:T(8,128)(2,1)} copy(bf16[64,8,128]{2,1,0:T(8,128)(2,1)S(1)} %conv_gather.1) | data formatting | bytes 262144

commit v4 on v3

--- a/solution.py
+++ b/solution.py
@@ -10,37 +10,41 @@
 MESH = pl.DeviceIdType.MESH
 PARTS = 2
 PLAN = [
+    ('turn', 0),
+    ('turn', 1),
+    ('send', (0, 0), 0, (0, 2)),
     ('send', (0, 0), 0, (1, 0)),
+    ('send', (0, 0), 1, (0, 2)),
+    ('send', (0, 0), 1, (1, 0)),
     ('send', (0, 0), 1, (0, 1)),
     ('send', (0, 0), 0, (0, 3)),
-    ('send', (0, 0), 1, (1, 0)),
     ('send', (0, 0), 0, (0, 1)),
     ('send', (0, 0), 1, (0, 3)),
-    ('send', (0, 0), 0, (1, 2)),
-    ('send', (0, 0), 1, (1, 2)),
     ('own',),
-    ('wait', (0, 1), 1),
-    ('send', (0, 1), 1, (0, 3)),
-    ('send', (0, 1), 1, (1, 0)),
-    ('wait', (0, 3), 0),
-    ('send', (0, 3), 0, (0, 1)),
-    ('send', (0, 3), 0, (1, 0)),
+    ('wait', (0, 2), 0),
+    ('send', (0, 2), 0, (1, 0)),
     ('wait', (1, 0), 0),
     ('send', (1, 0), 0, (0, 1)),
+    ('send', (1, 0), 0, (0, 3)),
+    ('wait', (0, 2), 1),
+    ('send', (0, 2), 1, (1, 0)),
     ('wait', (1, 0), 1),
+    ('send', (1, 0), 1, (0, 1)),
     ('send', (1, 0), 1, (0, 3)),
     ('wait', (0, 1), 0),
+    ('wait', (0, 1), 1),
+    ('first', (0, 0)),
+    ('wait', (0, 3), 0),
     ('wait', (0, 3), 1),
-    ('wait', (0, 2), 0),
-    ('wait', (0, 2), 1),
-    ('first',),
+    ('next', (0, 2)),
     ('wait', (1, 1), 0),
+    ('wait', (1, 1), 1),
+    ('next', (1, 0)),
     ('wait', (1, 3), 0),
-    ('wait', (1, 1), 1),
     ('wait', (1, 3), 1),
     ('wait', (1, 2), 0),
     ('wait', (1, 2), 1),
-    ('second',),
+    ('last', (1, 2)),
 ]
 F32 = jnp.float32
 BF16 = jnp.bfloat16
@@ -72,10 +76,13 @@
     def exists(dx, dy):
         return has_x[dx] & has_y[dy]
 
-    load_v = pltpu.make_async_copy(v_hbm, V, load_sem.at[0])
-    load_w = pltpu.make_async_copy(w_hbm, W, load_sem.at[1])
-    load_b = pltpu.make_async_copy(b_hbm, B, load_sem.at[2])
-    load_v.start()
+    step_ch = cin // PARTS
+    load_v = [pltpu.make_async_copy(v_hbm.at[pl.ds(p * step_ch, step_ch)], V.at[pl.ds(p * step_ch, step_ch)],
+                                    load_sem.at[2 + p]) for p in range(PARTS)]
+    load_w = pltpu.make_async_copy(w_hbm, W, load_sem.at[0])
+    load_b = pltpu.make_async_copy(b_hbm, B, load_sem.at[1])
+    for load in load_v:
+        load.start()
     load_b.start()
     load_w.start()
 
@@ -94,34 +101,29 @@
     across_y = jnp.where(has_y[-1], 1, 0) + jnp.where(has_y[1], 1, 0) + 1
     n_spots = across_x * across_y - 1
 
-    lane = lax.broadcasted_iota(jnp.int32, (cin, LANES), 1)
+    lane = lax.broadcasted_iota(jnp.int32, (step_ch, LANES), 1)
     z = lax.rem(lane, CZ)
 
-    load_v.wait()
-    flat[...] = V[...].astype(F32).reshape(cin * cells_x, LANES)
-
-    def rows(who):
-        return pl.ds(pl.multiple_of(who * cin, cin), cin)
-
-    zero = jnp.zeros((group * 2, LANES), BF16)
-    for c in range(3):
-        X[c, 0] = zero
-        X[c, cells_x + 1] = zero
-
-    mine = rows(ch)
-    for x in range(cells_x):
-        X[1, x + 1, mine, :] = flat[pl.ds(x, cin, stride=cells_x), :].astype(BF16)
-
-    def shift_z(who, xs):
-        r = rows(who)
-        for x in xs:
-            v = X[1, x + 1, r, :]
-            X[0, x + 1, r, :] = jnp.where(z == 0, jnp.zeros_like(v), pltpu.roll(v, 1, 1))
-            X[2, x + 1, r, :] = jnp.where(z == CZ - 1, jnp.zeros_like(v), pltpu.roll(v, LANES - 1, 1))
+    def rows(who, part):
+        return pl.ds(pl.multiple_of(who * cin + part * step_ch, step_ch), step_ch)
+
+    def turn(part):
+        load_v[part].wait()
+        n = step_ch * cells_x
+        flat[part * n : (part + 1) * n] = V[pl.ds(part * step_ch, step_ch)].astype(F32).reshape(n, LANES)
+        for x in range(cells_x):
+            piece = flat[pl.ds(part * n + x, step_ch, stride=cells_x), :]
+            X[1, x + 1, rows(ch, part), :] = piece.astype(BF16)
+
+    def shift_z(who, part):
+        r = rows(who, part)
+        for x in range(1, cells_x + 1):
+            v = X[1, x, r, :]
+            X[0, x, r, :] = jnp.where(z == 0, jnp.zeros_like(v), pltpu.roll(v, 1, 1))
+            X[2, x, r, :] = jnp.where(z == CZ - 1, jnp.zeros_like(v), pltpu.roll(v, LANES - 1, 1))
 
     def block_copy(block, part, out, slot, to):
-        width = cells_x // PARTS
-        piece = X.at[1, 1 + part * width : 1 + (part + 1) * width, rows(member(*block)), :]
+        piece = X.at[1, 1 : cells_x + 1, rows(member(*block), part), :]
         return pltpu.make_async_remote_copy(
             src_ref=piece, dst_ref=piece, send_sem=gs.at[out], recv_sem=gr.at[slot],
             device_id=mate(*to), device_id_type=MESH)
@@ -137,39 +139,54 @@
     def arrived(block, part):
         block_copy(block, part, 0, (block[0] * half_ch + block[1]) * PARTS + part, (1, 0)).wait_recv()
 
-    def products(which, first):
-        cols = pl.ds(pl.multiple_of(which * group, group), group)
-        for p in range((cells_x + 2) // 2):
+    pair = 2 * cin
+    n_pairs = (cells_x + 2) // 2
+
+    def products(block, first, rows_of, spans):
+        cols = pl.ds(pl.multiple_of(member(*block) // 2 * pair, pair), pair)
+        for p in spans:
             taps = [a for a in range(3) if 0 < 2 * p + a and 2 * p + a - 1 < cells_x + 1]
             lhs = jnp.concatenate(
-                [W[a, :, c, :, cols].reshape(3 * cout, group) for a in taps for c in range(3)], axis=1)
+                [jnp.concatenate([W[a, b, c, :, cols] for b in rows_of], axis=0) for a in taps for c in range(3)],
+                axis=1)
             rhs = jnp.concatenate(
                 [jnp.concatenate([X[c, 2 * p + a - 1, cols, :], X[c, 2 * p + a, cols, :]], axis=1)
                  for a in taps for c in range(3)], axis=0)
             r = jnp.dot(lhs, rhs, preferred_element_type=F32)
             for j in range(2):
-                part = r[:, LANES * j : LANES * (j + 1)]
-                if first:
-                    acc[2 * p + j] = part
-                else:
-                    acc[2 * p + j] = acc[2 * p + j] + part
-
-    pl.semaphore_wait(barrier, len(mates) + n_spots)
+                for i, b in enumerate(rows_of):
+                    part = r[i * cout : (i + 1) * cout, LANES * j : LANES * (j + 1)]
+                    spot = slice(b * cout, (b + 1) * cout)
+                    acc[2 * p + j, spot] = part if first else acc[2 * p + j, spot] + part
+
+    ready = False
     for step in PLAN:
-        if step[0] == "send":
+        if step[0] == "turn":
+            turn(step[1])
+        elif step[0] == "send":
+            if not ready:
+                pl.semaphore_wait(barrier, len(mates) + n_spots)
+                ready = True
             send(*step[1:])
         elif step[0] == "wait":
             arrived(*step[1:])
-            width = cells_x // PARTS
-            shift_z(member(*step[1]), range(step[2] * width, (step[2] + 1) * width))
+            shift_z(member(*step[1]), step[2])
         elif step[0] == "own":
-            shift_z(ch, range(cells_x))
+            zero = jnp.zeros((n_ch * cin, LANES), BF16)
+            for c in range(3):
+                X[c, 0] = zero
+                X[c, cells_x + 1] = zero
+            for part in range(PARTS):
+                shift_z(ch, part)
         elif step[0] == "first":
             load_w.wait()
             load_b.wait()
-            products(h, True)
+            products(step[1], True, (0, 1, 2), range(n_pairs))
+        elif step[0] == "next":
+            products(step[1], False, (0, 1, 2), range(n_pairs))
         else:
-            products(1 - h, False)
+            products(step[1], False, (0, 1, 2), (0, n_pairs - 1))
+            products(step[1], False, (0, 2), range(1, n_pairs - 1))
 
     lane_o = lax.broadcasted_iota(jnp.int32, (cout, LANES), 1)
     last = LANES - CZ
@@ -186,8 +203,6 @@
         by = by % LANES
         return pltpu.roll(v, by, 1) if by else v
 
-    hx[0] = along_y(0)
-    hx[1] = along_y(cells_x + 1)
     low = jnp.zeros((cout, LANES), F32)
     high = jnp.zeros((cout, LANES), F32)
     for x in range(cells_x):
@@ -196,17 +211,6 @@
         high = jnp.where(here, roll(taps_of(x + 1, 0), x * CZ - last), high)
     hy[0] = low
     hy[1] = high
-    rows_of = cout // 8
-    lane_8 = lax.broadcasted_iota(jnp.int32, (8, LANES), 1)
-    for i, s in enumerate((0, cells_x + 1)):
-        for j, (b, start) in enumerate(((2, 0), (0, last))):
-            corner = jnp.zeros((8, LANES), F32)
-            for g in range(rows_of):
-                here = (lane_8 >= g * CZ) & (lane_8 < (g + 1) * CZ)
-                piece = acc[s, b * cout + 8 * g : b * cout + 8 * g + 8]
-                corner = jnp.where(here, roll(piece, g * CZ - start), corner)
-            hc[2 * i + j] = corner
-
     edges = [(hy.at[0], ry.at[0], 0, -1), (hy.at[1], ry.at[1], 0, 1),
              (hx.at[0], rx.at[0], -1, 0), (hx.at[1], rx.at[1], 1, 0)]
     edges += [(hc.at[2 * i + j], rc.at[2 * i + j], dx, dy)
@@ -218,12 +222,31 @@
             src_ref=src, dst_ref=dst, send_sem=hs.at[k], recv_sem=hr.at[k],
             device_id=spatial(dx, dy), device_id_type=MESH)
 
-    for k, (_, _, dx, dy) in enumerate(edges):
-
-        @pl.when(exists(dx, dy))
-        def _():
-            edge_copy(k).start()
-
+    def leave(ks):
+        for k in ks:
+
+            @pl.when(exists(*edges[k][2:]))
+            def _():
+                edge_copy(k).start()
+
+    leave(range(2))
+    groups = cout // 8
+    lane_8 = lax.broadcasted_iota(jnp.int32, (8, LANES), 1)
+    for i, s in enumerate((0, cells_x + 1)):
+        for j, (b, start) in enumerate(((2, 0), (0, last))):
+            corner = jnp.zeros((8, LANES), F32)
+            for g in range(groups):
+                here = (lane_8 >= g * CZ) & (lane_8 < (g + 1) * CZ)
+                piece = acc[s, b * cout + 8 * g : b * cout + 8 * g + 8]
+                corner = jnp.where(here, roll(piece, g * CZ - start), corner)
+            hc[2 * i + j] = corner
+
+    leave(range(4, 8))
+    hx[0] = along_y(0)
+    hx[1] = along_y(cells_x + 1)
+    leave(range(2, 4))
+
+    products(PLAN[-1][1], False, (1,), range(1, n_pairs - 1))
     sub = lax.broadcasted_iota(jnp.int32, (cout, cout), 0)
     across = lax.broadcasted_iota(jnp.int32, (cout, cout), 1)
     bias = jnp.sum(jnp.where(sub == across, jnp.broadcast_to(B[...], (cout, cout)), 0.0),
@@ -251,7 +274,7 @@
             for j in range(2):
                 start = 0 if j == 0 else last
                 packed = jnp.where(has[i] & has_end[j], rc[2 * (1 - i) + 1 - j], jnp.zeros((8, LANES), F32))
-                spread = jnp.concatenate([roll(packed, start - g * CZ) for g in range(rows_of)], axis=0)
+                spread = jnp.concatenate([roll(packed, start - g * CZ) for g in range(groups)], axis=0)
                 inside = lane_o < CZ if j == 0 else lane_o >= last
                 extra = extra + jnp.where(inside, spread, 0.0)
         spot = pl.ds(x, cout, stride=cells_x)
@@ -296,7 +319,7 @@
                 pltpu.VMEM((2, cout, LANES), F32),
                 pltpu.VMEM((2, cout, LANES), F32),
                 pltpu.VMEM((4, 8, LANES), F32),
-                pltpu.SemaphoreType.DMA((3,)),
+                pltpu.SemaphoreType.DMA((2 + PARTS,)),
                 pltpu.SemaphoreType.DMA((n_ch * PARTS,)),
                 pltpu.SemaphoreType.DMA((n_ch * PARTS,)),
                 pltpu.SemaphoreType.DMA((8,)),

time: 24.8 us -> 22.9 us (0.923)
  Pallas kernels: 24 us -> 22 us
    pallas_call x1, Pallas kernels: 24 us -> 22 us  [per_device(): call(*[pltpu.with_memory_space_constraint(a, pltpu.HBM) for a in (volume,...]
where the time goes in v4:
time: 22.9 us; the launch traced here: 22.6 us
  Pallas kernels  22 us (96%)
  local copies, waits for them, and re-layouts  0.66 us (3%)
    pallas_call x1, Pallas kernels, per_device(): call(*[pltpu.with_memory_space_constraint(a, pltpu.HBM) for a in (volume,...  22 us
    unnamed x1, local copies, waits for them, and re-layouts  0.66 us

profile of v4, /device:TPU:97, one launch (start us, length us, event | category | flops | bytes accessed | tf_op | source)
XLA Modules:
  0.0 22.6 jit_solution(16923313375888579070)
XLA Ops:
  0.0 22.0 %conv_gather.1 = bf16[64,8,128]{2,1,0:T(8,128)(2,1)S(1)} custom-call(bf16[64,8,128]{2,1,0:T(8,128)(2,1)} %refs_0_.1, bf16[3,3,3,64,512]{4,3,2,1,0:T(8,128)(2,1)} %refs_1_.1, f32[1,64]{1,0:T(1,128)} %bitcast.1), custom_call_target="tpu_custom_call" | custom-call | tf_op jit(solution)/shard_map/conv_gather/pallas_call | solution.py:332
  22.0 0.7 %copy.5 = bf16[64,8,128]{2,1,0:T(8,128)(2,1)} copy(bf16[64,8,128]{2,1,0:T(8,128)(2,1)S(1)} %conv_gather.1) | data formatting | bytes 262144

commit v5 on v4

--- a/solution.py
+++ b/solution.py
@@ -12,10 +12,10 @@
 PLAN = [
     ('turn', 0),
     ('turn', 1),
+    ('send', (0, 0), 0, (1, 0)),
     ('send', (0, 0), 0, (0, 2)),
-    ('send', (0, 0), 0, (1, 0)),
+    ('send', (0, 0), 1, (1, 0)),
     ('send', (0, 0), 1, (0, 2)),
-    ('send', (0, 0), 1, (1, 0)),
     ('send', (0, 0), 1, (0, 1)),
     ('send', (0, 0), 0, (0, 3)),
     ('send', (0, 0), 0, (0, 1)),
@@ -51,7 +51,7 @@
 
 
 def kernel(sizes, v_hbm, w_hbm, b_hbm, o_ref, X, W, V, B, acc, flat, hx, hy, hc, rx, ry, rc,
-           load_sem, gs, gr, hs, hr):
+           load_sem, gs, gr, hs, hr, entered):
     n_sx, n_sy, n_ch = sizes
     half_ch = n_ch // 2
     cin, cells_x = V.shape[0], V.shape[1]
@@ -88,18 +88,22 @@
 
     barrier = pltpu.get_barrier_semaphore()
     mates = sorted({step[3] for step in PLAN if step[0] == "send"})
-    spots = [(dx, dy) for dx in (-1, 0, 1) for dy in (-1, 0, 1) if (dx, dy) != (0, 0)]
+    later = [(0, 1), (-1, 1), (1, 1), (1, 0)]
+    earlier = [(-dx, -dy) for dx, dy in later]
     for m in mates:
         pl.semaphore_signal(barrier, inc=1, device_id=mate(*m), device_id_type=MESH)
-    for s in spots:
-
-        @pl.when(exists(*s))
-        def _():
-            pl.semaphore_signal(barrier, inc=1, device_id=spatial(*s), device_id_type=MESH)
-
-    across_x = jnp.where(has_x[-1], 1, 0) + jnp.where(has_x[1], 1, 0) + 1
-    across_y = jnp.where(has_y[-1], 1, 0) + jnp.where(has_y[1], 1, 0) + 1
-    n_spots = across_x * across_y - 1
+
+    def tell(sem, places):
+        for place in places:
+
+            @pl.when(exists(*place))
+            def _():
+                pl.semaphore_signal(sem, inc=1, device_id=spatial(*place), device_id_type=MESH)
+
+    def count(places):
+        return sum(jnp.where(exists(*place), 1, 0) for place in places)
+
+    tell(barrier, later)
 
     lane = lax.broadcasted_iota(jnp.int32, (step_ch, LANES), 1)
     z = lax.rem(lane, CZ)
@@ -165,13 +169,14 @@
             turn(step[1])
         elif step[0] == "send":
             if not ready:
-                pl.semaphore_wait(barrier, len(mates) + n_spots)
+                pl.semaphore_wait(barrier, len(mates) + count(earlier))
                 ready = True
             send(*step[1:])
         elif step[0] == "wait":
             arrived(*step[1:])
             shift_z(member(*step[1]), step[2])
         elif step[0] == "own":
+            tell(entered, earlier)
             zero = jnp.zeros((n_ch * cin, LANES), BF16)
             for c in range(3):
                 X[c, 0] = zero
@@ -228,6 +233,12 @@
             @pl.when(exists(*edges[k][2:]))
             def _():
                 edge_copy(k).start()
+
+    some = count(later)
+
+    @pl.when(some > 0)
+    def _():
+        pl.semaphore_wait(entered, some)
 
     leave(range(2))
     groups = cout // 8
@@ -324,6 +335,7 @@
                 pltpu.SemaphoreType.DMA((n_ch * PARTS,)),
                 pltpu.SemaphoreType.DMA((8,)),
                 pltpu.SemaphoreType.DMA((8,)),
+                pltpu.SemaphoreType.REGULAR,
             ],
             compiler_params=pltpu.CompilerParams(
                 collective_id=0, has_side_effects=True, vmem_limit_bytes=32 << 20),

time: 22.9 us -> 22.7 us (level)
  no operation moved by 1% of the time
where the time goes in v5:
time: 22.7 us; the launch traced here: 22.6 us
  Pallas kernels  22 us (97%)
  local copies, waits for them, and re-layouts  0.66 us (3%)
    pallas_call x1, Pallas kernels, per_device(): call(*[pltpu.with_memory_space_constraint(a, pltpu.HBM) for a in (volume,...  22 us
    unnamed x1, local copies, waits for them, and re-layouts  0.66 us

profile of v5, /device:TPU:97, one launch (start us, length us, event | category | flops | bytes accessed | tf_op | source)
XLA Modules:
  0.0 22.6 jit_solution(3217127513729615654)
XLA Ops:
  0.0 22.0 %conv_gather.1 = bf16[64,8,128]{2,1,0:T(8,128)(2,1)S(1)} custom-call(bf16[64,8,128]{2,1,0:T(8,128)(2,1)} %refs_0_.1, bf16[3,3,3,64,512]{4,3,2,1,0:T(8,128)(2,1)} %refs_1_.1, f32[1,64]{1,0:T(1,128)} %bitcast.1), custom_call_target="tpu_custom_call" | custom-call | tf_op jit(solution)/shard_map/conv_gather/pallas_call | solution.py:344
  22.0 0.7 %copy.5 = bf16[64,8,128]{2,1,0:T(8,128)(2,1)} copy(bf16[64,8,128]{2,1,0:T(8,128)(2,1)S(1)} %conv_gather.1) | data formatting | bytes 262144

commit v6 on v5

--- a/solution.py
+++ b/solution.py
@@ -37,20 +37,20 @@
     ('wait', (0, 3), 0),
     ('wait', (0, 3), 1),
     ('next', (0, 2)),
+    ('ends',),
     ('wait', (1, 1), 0),
     ('wait', (1, 1), 1),
-    ('next', (1, 0)),
     ('wait', (1, 3), 0),
     ('wait', (1, 3), 1),
     ('wait', (1, 2), 0),
     ('wait', (1, 2), 1),
-    ('last', (1, 2)),
+    ('last',),
 ]
 F32 = jnp.float32
 BF16 = jnp.bfloat16
 
 
-def kernel(sizes, v_hbm, w_hbm, b_hbm, o_ref, X, W, V, B, acc, flat, hx, hy, hc, rx, ry, rc,
+def kernel(sizes, v_hbm, w_hbm, b_hbm, o_ref, X, W, V, B, acc, ends, flat, hx, hy, hc, rx, ry, rc,
            load_sem, gs, gr, hs, hr, entered):
     n_sx, n_sy, n_ch = sizes
     half_ch = n_ch // 2
@@ -126,6 +126,31 @@
             X[0, x, r, :] = jnp.where(z == 0, jnp.zeros_like(v), pltpu.roll(v, 1, 1))
             X[2, x, r, :] = jnp.where(z == CZ - 1, jnp.zeros_like(v), pltpu.roll(v, LANES - 1, 1))
 
+    last = LANES - CZ
+    along_x = lane // CZ
+    valid_x = (along_x >= 1, None, along_x < cells_x - 1)
+    valid_z = (z >= 1, None, z < CZ - 1)
+
+    def roll(v, by):
+        by = by % LANES
+        return pltpu.roll(v, by, 1) if by else v
+
+    def pack_ends(block, part):
+        r = rows(member(*block), part)
+        within = lax.rem(member(*block), half_ch) * cin + part * step_ch
+        to = pl.ds(pl.multiple_of(within, step_ch), step_ch)
+        for e, start in enumerate((0, last)):
+            packed = jnp.zeros((step_ch, LANES), BF16)
+            for x in range(cells_x):
+                packed = jnp.where(along_x == x, roll(X[1, x + 1, r, :], x * CZ - start), packed)
+            for a in range(3):
+                for c in range(3):
+                    v = roll(packed, (1 - a) * CZ + 1 - c)
+                    for valid in (valid_x[a], valid_z[c]):
+                        if valid is not None:
+                            v = jnp.where(valid, v, jnp.zeros_like(v))
+                    ends[e, 3 * a + c, to, :] = v
+
     def block_copy(block, part, out, slot, to):
         piece = X.at[1, 1 : cells_x + 1, rows(member(*block), part), :]
         return pltpu.make_async_remote_copy(
@@ -144,24 +169,83 @@
         block_copy(block, part, 0, (block[0] * half_ch + block[1]) * PARTS + part, (1, 0)).wait_recv()
 
     pair = 2 * cin
-    n_pairs = (cells_x + 2) // 2
-
-    def products(block, first, rows_of, spans):
-        cols = pl.ds(pl.multiple_of(member(*block) // 2 * pair, pair), pair)
-        for p in spans:
-            taps = [a for a in range(3) if 0 < 2 * p + a and 2 * p + a - 1 < cells_x + 1]
+
+    def pair_of(block):
+        return pl.ds(pl.multiple_of(member(*block) // 2 * pair, pair), pair)
+
+    ends_x = [(0,), (cells_x + 1,)]
+    inside = [(x, x + 1) for x in range(1, cells_x + 1, 2)]
+
+    def products(cols, first, spans):
+        for slabs in spans:
+            taps = [a for a in range(3) if any(0 < o + a - 1 < cells_x + 1 for o in slabs)]
             lhs = jnp.concatenate(
-                [jnp.concatenate([W[a, b, c, :, cols] for b in rows_of], axis=0) for a in taps for c in range(3)],
-                axis=1)
+                [W[a, :, c, :, cols].reshape(3 * cout, cols.size) for a in taps for c in range(3)], axis=1)
             rhs = jnp.concatenate(
-                [jnp.concatenate([X[c, 2 * p + a - 1, cols, :], X[c, 2 * p + a, cols, :]], axis=1)
+                [jnp.concatenate([X[c, o + a - 1, cols, :] for o in slabs], axis=1)
                  for a in taps for c in range(3)], axis=0)
             r = jnp.dot(lhs, rhs, preferred_element_type=F32)
-            for j in range(2):
-                for i, b in enumerate(rows_of):
-                    part = r[i * cout : (i + 1) * cout, LANES * j : LANES * (j + 1)]
-                    spot = slice(b * cout, (b + 1) * cout)
-                    acc[2 * p + j, spot] = part if first else acc[2 * p + j, spot] + part
+            for j, o in enumerate(slabs):
+                part = r[:, LANES * j : LANES * (j + 1)]
+                acc[o] = part if first else acc[o] + part
+
+    lane_o = lax.broadcasted_iota(jnp.int32, (cout, LANES), 1)
+
+    def taps_of(s, b):
+        return acc[s, b * cout : (b + 1) * cout]
+
+    def along_y(s):
+        up = jnp.where(lane_o < CZ, 0.0, pltpu.roll(taps_of(s, 0), CZ, 1))
+        down = jnp.where(lane_o >= last, 0.0, pltpu.roll(taps_of(s, 2), LANES - CZ, 1))
+        return taps_of(s, 1) + up + down
+
+    groups = cout // 8
+    lane_8 = lax.broadcasted_iota(jnp.int32, (8, LANES), 1)
+    def corners():
+        for i, s in enumerate((0, cells_x + 1)):
+            for j, (b, start) in enumerate(((2, 0), (0, last))):
+                corner = jnp.zeros((8, LANES), F32)
+                for g in range(groups):
+                    here = (lane_8 >= g * CZ) & (lane_8 < (g + 1) * CZ)
+                    piece = acc[s, b * cout + 8 * g : b * cout + 8 * g + 8]
+                    corner = jnp.where(here, roll(piece, g * CZ - start), corner)
+                hc[2 * i + j] = corner
+
+    def ends_so_far():
+        low = jnp.zeros((cout, LANES), F32)
+        high = jnp.zeros((cout, LANES), F32)
+        for x in range(cells_x):
+            here = (lane_o >= x * CZ) & (lane_o < (x + 1) * CZ)
+            low = jnp.where(here, roll(taps_of(x + 1, 2), x * CZ), low)
+            high = jnp.where(here, roll(taps_of(x + 1, 0), x * CZ - last), high)
+        hy[0] = low
+        hy[1] = high
+
+    far_half = pl.ds(pl.multiple_of((1 - h) * group, group), group)
+
+    def ends_of(cols):
+        for e, b in enumerate((2, 0)):
+            lhs = jnp.concatenate([W[a, b, c, :, cols] for a in range(3) for c in range(3)], axis=1)
+            rhs = jnp.concatenate([ends[e, t] for t in range(9)], axis=0)
+            hy[e] = hy[e] + jnp.dot(lhs, rhs, preferred_element_type=F32)
+
+    edges = [(hy.at[0], ry.at[0], 0, -1), (hy.at[1], ry.at[1], 0, 1),
+             (hx.at[0], rx.at[0], -1, 0), (hx.at[1], rx.at[1], 1, 0)]
+    edges += [(hc.at[2 * i + j], rc.at[2 * i + j], dx, dy)
+              for i, dx in enumerate((-1, 1)) for j, dy in enumerate((-1, 1))]
+
+    def edge_copy(k):
+        src, dst, dx, dy = edges[k]
+        return pltpu.make_async_remote_copy(
+            src_ref=src, dst_ref=dst, send_sem=hs.at[k], recv_sem=hr.at[k],
+            device_id=spatial(dx, dy), device_id_type=MESH)
+
+    def leave(ks):
+        for k in ks:
+
+            @pl.when(exists(*edges[k][2:]))
+            def _():
+                edge_copy(k).start()
 
     ready = False
     for step in PLAN:
@@ -174,7 +258,12 @@
             send(*step[1:])
         elif step[0] == "wait":
             arrived(*step[1:])
-            shift_z(member(*step[1]), step[2])
+            if step[1][0] == 1:
+                pack_ends(*step[1:])
+            if step[1] != (1, 2):
+                shift_z(member(*step[1]), step[2])
+        elif step[0] == "ends":
+            ends_so_far()
         elif step[0] == "own":
             tell(entered, earlier)
             zero = jnp.zeros((n_ch * cin, LANES), BF16)
@@ -186,78 +275,29 @@
         elif step[0] == "first":
             load_w.wait()
             load_b.wait()
-            products(step[1], True, (0, 1, 2), range(n_pairs))
+            products(pair_of(step[1]), True, ends_x + inside)
         elif step[0] == "next":
-            products(step[1], False, (0, 1, 2), range(n_pairs))
+            products(pair_of(step[1]), False, ends_x + inside)
         else:
-            products(step[1], False, (0, 1, 2), (0, n_pairs - 1))
-            products(step[1], False, (0, 2), range(1, n_pairs - 1))
-
-    lane_o = lax.broadcasted_iota(jnp.int32, (cout, LANES), 1)
-    last = LANES - CZ
-
-    def taps_of(s, b):
-        return acc[s, b * cout : (b + 1) * cout]
-
-    def along_y(s):
-        up = jnp.where(lane_o < CZ, 0.0, pltpu.roll(taps_of(s, 0), CZ, 1))
-        down = jnp.where(lane_o >= last, 0.0, pltpu.roll(taps_of(s, 2), LANES - CZ, 1))
-        return taps_of(s, 1) + up + down
-
-    def roll(v, by):
-        by = by % LANES
-        return pltpu.roll(v, by, 1) if by else v
-
-    low = jnp.zeros((cout, LANES), F32)
-    high = jnp.zeros((cout, LANES), F32)
-    for x in range(cells_x):
-        here = (lane_o >= x * CZ) & (lane_o < (x + 1) * CZ)
-        low = jnp.where(here, roll(taps_of(x + 1, 2), x * CZ), low)
-        high = jnp.where(here, roll(taps_of(x + 1, 0), x * CZ - last), high)
-    hy[0] = low
-    hy[1] = high
-    edges = [(hy.at[0], ry.at[0], 0, -1), (hy.at[1], ry.at[1], 0, 1),
-             (hx.at[0], rx.at[0], -1, 0), (hx.at[1], rx.at[1], 1, 0)]
-    edges += [(hc.at[2 * i + j], rc.at[2 * i + j], dx, dy)
-              for i, dx in enumerate((-1, 1)) for j, dy in enumerate((-1, 1))]
-
-    def edge_copy(k):
-        src, dst, dx, dy = edges[k]
-        return pltpu.make_async_remote_copy(
-            src_ref=src, dst_ref=dst, send_sem=hs.at[k], recv_sem=hr.at[k],
-            device_id=spatial(dx, dy), device_id_type=MESH)
-
-    def leave(ks):
-        for k in ks:
-
-            @pl.when(exists(*edges[k][2:]))
+            ends_of(far_half)
+            some = count(later)
+
+            @pl.when(some > 0)
             def _():
-                edge_copy(k).start()
-
-    some = count(later)
-
-    @pl.when(some > 0)
-    def _():
-        pl.semaphore_wait(entered, some)
-
-    leave(range(2))
-    groups = cout // 8
-    lane_8 = lax.broadcasted_iota(jnp.int32, (8, LANES), 1)
-    for i, s in enumerate((0, cells_x + 1)):
-        for j, (b, start) in enumerate(((2, 0), (0, last))):
-            corner = jnp.zeros((8, LANES), F32)
-            for g in range(groups):
-                here = (lane_8 >= g * CZ) & (lane_8 < (g + 1) * CZ)
-                piece = acc[s, b * cout + 8 * g : b * cout + 8 * g + 8]
-                corner = jnp.where(here, roll(piece, g * CZ - start), corner)
-            hc[2 * i + j] = corner
-
-    leave(range(4, 8))
-    hx[0] = along_y(0)
-    hx[1] = along_y(cells_x + 1)
-    leave(range(2, 4))
-
-    products(PLAN[-1][1], False, (1,), range(1, n_pairs - 1))
+                pl.semaphore_wait(entered, some)
+
+            leave(range(2))
+            for part in range(PARTS):
+                shift_z(member(1, 2), part)
+            products(far_half, False, ends_x)
+            corners()
+            leave(range(4, 8))
+            hx[0] = along_y(0)
+            hx[1] = along_y(cells_x + 1)
+            leave(range(2, 4))
+
+
+    products(far_half, False, inside)
     sub = lax.broadcasted_iota(jnp.int32, (cout, cout), 0)
     across = lax.broadcasted_iota(jnp.int32, (cout, cout), 1)
     bias = jnp.sum(jnp.where(sub == across, jnp.broadcast_to(B[...], (cout, cout)), 0.0),
@@ -323,6 +363,7 @@
                 pltpu.VMEM((cin, cells_x, LANES), BF16),
                 pltpu.VMEM((1, cout), F32),
                 pltpu.VMEM((cells_x + 2, 3 * cout, LANES), F32),
+                pltpu.VMEM((2, 9, n_ch // 2 * cin, LANES), BF16),
                 pltpu.VMEM((cout * cells_x, LANES), F32),
                 pltpu.VMEM((2, cout, LANES), F32),
                 pltpu.VMEM((2, cout, LANES), F32),

time: 22.7 us -> 22.6 us (level)
  no operation moved by 1% of the time
where the time goes in v6:
time: 22.6 us; the launch traced here: 22.5 us
  Pallas kernels  21.9 us (97%)
  local copies, waits for them, and re-layouts  0.66 us (3%)
    pallas_call x1, Pallas kernels, per_device(): call(*[pltpu.with_memory_space_constraint(a, pltpu.HBM) for a in (volume,...  21.9 us
    unnamed x1, local copies, waits for them, and re-layouts  0.66 us

profile of v6, /device:TPU:97, one launch (start us, length us, event | category | flops | bytes accessed | tf_op | source)
XLA Modules:
  0.0 22.5 jit_solution(4917855223477405616)
XLA Ops:
  0.0 21.9 %conv_gather.1 = bf16[64,8,128]{2,1,0:T(8,128)(2,1)S(1)} custom-call(bf16[64,8,128]{2,1,0:T(8,128)(2,1)} %refs_0_.1, bf16[3,3,3,64,512]{4,3,2,1,0:T(8,128)(2,1)} %refs_1_.1, f32[1,64]{1,0:T(1,128)} %bitcast.1), custom_call_target="tpu_custom_call" | custom-call | tf_op jit(solution)/shard_map/conv_gather/pallas_call | solution.py:385
  21.9 0.7 %copy.5 = bf16[64,8,128]{2,1,0:T(8,128)(2,1)} copy(bf16[64,8,128]{2,1,0:T(8,128)(2,1)S(1)} %conv_gather.1) | data formatting | bytes 262144

commit v7 on v6

--- a/solution.py
+++ b/solution.py
@@ -11,9 +11,9 @@
 PARTS = 2
 PLAN = [
     ('turn', 0),
-    ('turn', 1),
     ('send', (0, 0), 0, (1, 0)),
     ('send', (0, 0), 0, (0, 2)),
+    ('turn', 1),
     ('send', (0, 0), 1, (1, 0)),
     ('send', (0, 0), 1, (0, 2)),
     ('send', (0, 0), 1, (0, 1)),

time: 22.6 us -> 22.7 us (level)
  no operation moved by 1% of the time
where the time goes in v7:
time: 22.7 us; the launch traced here: 22.6 us
  Pallas kernels  21.9 us (96%)
  local copies, waits for them, and re-layouts  0.66 us (3%)
    pallas_call x1, Pallas kernels, per_device(): call(*[pltpu.with_memory_space_constraint(a, pltpu.HBM) for a in (volume,...  21.9 us
    unnamed x1, local copies, waits for them, and re-layouts  0.66 us

profile of v7, /device:TPU:97, one launch (start us, length us, event | category | flops | bytes accessed | tf_op | source)
XLA Modules:
  0.0 22.6 jit_solution(13439593346745636112)
XLA Ops:
  0.0 21.9 %conv_gather.1 = bf16[64,8,128]{2,1,0:T(8,128)(2,1)S(1)} custom-call(bf16[64,8,128]{2,1,0:T(8,128)(2,1)} %refs_0_.1, bf16[3,3,3,64,512]{4,3,2,1,0:T(8,128)(2,1)} %refs_1_.1, f32[1,64]{1,0:T(1,128)} %bitcast.1), custom_call_target="tpu_custom_call" | custom-call | tf_op jit(solution)/shard_map/conv_gather/pallas_call | solution.py:385
  21.9 0.7 %copy.5 = bf16[64,8,128]{2,1,0:T(8,128)(2,1)} copy(bf16[64,8,128]{2,1,0:T(8,128)(2,1)S(1)} %conv_gather.1) | data formatting | bytes 262144

commit v8 on v6

--- a/solution.py
+++ b/solution.py
@@ -305,31 +305,32 @@
     for x in range(cells_x):
         flat[pl.ds(x, cout, stride=cells_x), :] = along_y(x + 1) + bias
 
-    for k, (_, _, dx, dy) in enumerate(edges):
-
-        @pl.when(exists(-dx, -dy))
-        def _():
-            edge_copy(k).wait_recv()
-
     has, has_end = (has_x[-1], has_x[1]), (has_y[-1], has_y[1])
     zeros = jnp.zeros((cout, LANES), F32)
-    from_low_y = jnp.where(has_end[0], ry[1], zeros)
-    from_high_y = jnp.where(has_end[1], ry[0], zeros)
-    for x in range(cells_x):
-        extra = jnp.where(lane_o < CZ, roll(from_low_y, -x * CZ), 0.0)
-        extra = jnp.where(lane_o >= last, roll(from_high_y, last - x * CZ), extra)
-        if x in (0, cells_x - 1):
-            i = 0 if x == 0 else 1
-            extra = extra + jnp.where(has[i], rx[1 - i], zeros)
-            corners = []
-            for j in range(2):
-                start = 0 if j == 0 else last
+
+    def take(ks):
+        for k in ks:
+
+            @pl.when(exists(-edges[k][2], -edges[k][3]))
+            def _():
+                edge_copy(k).wait_recv()
+
+    for j, ks in enumerate(((1, 2, 3, 5, 7), (0, 4, 6))):
+        take(ks)
+        start = (0, last)[j]
+        inside_y = (lane_o < CZ, lane_o >= last)[j]
+        beyond = jnp.where(has_end[j], ry[1 - j], zeros)
+        for x in range(cells_x):
+            extra = jnp.where(inside_y, roll(beyond, start - x * CZ), 0.0)
+            if x in (0, cells_x - 1):
+                i = 0 if x == 0 else 1
                 packed = jnp.where(has[i] & has_end[j], rc[2 * (1 - i) + 1 - j], jnp.zeros((8, LANES), F32))
                 spread = jnp.concatenate([roll(packed, start - g * CZ) for g in range(groups)], axis=0)
-                inside = lane_o < CZ if j == 0 else lane_o >= last
-                extra = extra + jnp.where(inside, spread, 0.0)
-        spot = pl.ds(x, cout, stride=cells_x)
-        flat[spot, :] = flat[spot, :] + extra
+                extra = extra + jnp.where(inside_y, spread, 0.0)
+                if j == 0:
+                    extra = extra + jnp.where(has[i], rx[1 - i], zeros)
+            spot = pl.ds(x, cout, stride=cells_x)
+            flat[spot, :] = flat[spot, :] + extra
     o_ref[...] = flat[...].reshape(cout, cells_x, LANES).astype(BF16)
     for k, (_, _, dx, dy) in enumerate(edges):
 

time: 22.6 us -> 22.5 us (level)
  no operation moved by 1% of the time
where the time goes in v8:
time: 22.5 us
  Pallas kernels  21.8 us (97%)
  local copies, waits for them, and re-layouts  0.66 us (3%)
    pallas_call x1, Pallas kernels, per_device(): call(*[pltpu.with_memory_space_constraint(a, pltpu.HBM) for a in (volume,...  21.8 us
    unnamed x1, local copies, waits for them, and re-layouts  0.66 us

profile of v8, /device:TPU:97, one launch (start us, length us, event | category | flops | bytes accessed | tf_op | source)
XLA Modules:
  0.0 22.5 jit_solution(7493034887591419839)
XLA Ops:
  0.0 21.8 %conv_gather.1 = bf16[64,8,128]{2,1,0:T(8,128)(2,1)S(1)} custom-call(bf16[64,8,128]{2,1,0:T(8,128)(2,1)} %refs_0_.1, bf16[3,3,3,64,512]{4,3,2,1,0:T(8,128)(2,1)} %refs_1_.1, f32[1,64]{1,0:T(1,128)} %bitcast.1), custom_call_target="tpu_custom_call" | custom-call | tf_op jit(solution)/shard_map/conv_gather/pallas_call | solution.py:386
  21.8 0.7 %copy.5 = bf16[64,8,128]{2,1,0:T(8,128)(2,1)} copy(bf16[64,8,128]{2,1,0:T(8,128)(2,1)S(1)} %conv_gather.1) | data formatting | bytes 262144

commit v9 on v8

--- a/solution.py
+++ b/solution.py
@@ -11,9 +11,9 @@
 PARTS = 2
 PLAN = [
     ('turn', 0),
-    ('turn', 1),
     ('send', (0, 0), 0, (1, 0)),
     ('send', (0, 0), 0, (0, 2)),
+    ('turn', 1),
     ('send', (0, 0), 1, (1, 0)),
     ('send', (0, 0), 1, (0, 2)),
     ('send', (0, 0), 1, (0, 1)),
@@ -21,16 +21,16 @@
     ('send', (0, 0), 0, (0, 1)),
     ('send', (0, 0), 1, (0, 3)),
     ('own',),
-    ('wait', (0, 2), 0),
-    ('send', (0, 2), 0, (1, 0)),
     ('wait', (1, 0), 0),
     ('send', (1, 0), 0, (0, 1)),
     ('send', (1, 0), 0, (0, 3)),
-    ('wait', (0, 2), 1),
-    ('send', (0, 2), 1, (1, 0)),
+    ('wait', (0, 2), 0),
+    ('send', (0, 2), 0, (1, 0)),
     ('wait', (1, 0), 1),
     ('send', (1, 0), 1, (0, 1)),
     ('send', (1, 0), 1, (0, 3)),
+    ('wait', (0, 2), 1),
+    ('send', (0, 2), 1, (1, 0)),
     ('wait', (0, 1), 0),
     ('wait', (0, 1), 1),
     ('first', (0, 0)),

time: 22.5 us -> 22.6 us (level)
  no operation moved by 1% of the time
where the time goes in v9:
time: 22.6 us; the launch traced here: 22.5 us
  Pallas kernels  21.8 us (96%)
  local copies, waits for them, and re-layouts  0.66 us (3%)
    pallas_call x1, Pallas kernels, per_device(): call(*[pltpu.with_memory_space_constraint(a, pltpu.HBM) for a in (volume,...  21.8 us
    unnamed x1, local copies, waits for them, and re-layouts  0.66 us

profile of v9, /device:TPU:97, one launch (start us, length us, event | category | flops | bytes accessed | tf_op | source)
XLA Modules:
  0.0 22.5 jit_solution(9004448423719773146)
XLA Ops:
  0.0 21.8 %conv_gather.1 = bf16[64,8,128]{2,1,0:T(8,128)(2,1)S(1)} custom-call(bf16[64,8,128]{2,1,0:T(8,128)(2,1)} %refs_0_.1, bf16[3,3,3,64,512]{4,3,2,1,0:T(8,128)(2,1)} %refs_1_.1, f32[1,64]{1,0:T(1,128)} %bitcast.1), custom_call_target="tpu_custom_call" | custom-call | tf_op jit(solution)/shard_map/conv_gather/pallas_call | solution.py:386
  21.8 0.7 %copy.5 = bf16[64,8,128]{2,1,0:T(8,128)(2,1)} copy(bf16[64,8,128]{2,1,0:T(8,128)(2,1)S(1)} %conv_gather.1) | data formatting | bytes 262144
